TPU v7x, 512 devices: a whole 4x8x8 slice. The times are simulated.
512 devices in a mesh: grp: 16 (over y, core), seq: 32 (over z, x).
Axes of the slice: x: 4, y: 8, z: 8, core: 2. Of those that a mesh axis runs over, the one named last changes fastest.
Arguments:
- attention_output: bfloat16 [8192, 8192], P('grp', 'seq'), may hold values from -6 to 6
- output_gradient: bfloat16 [8192, 8192], P('grp', 'seq'), may hold values from -6 to 6
- output_projection_weight: bfloat16 [8192, 8192], P('seq', 'grp'), may hold values from -0.0625 to 0.0625
- tenant_down_factors: bfloat16 [32, 64, 8192], P(None, None, 'seq'), may hold values from -0.0625 to 0.0625
- tenant_up_factors: bfloat16 [32, 64, 8192], P(None, None, 'seq'), may hold values from -0.0625 to 0.0625
- block_tenant_index: int32 [64], replicated, may hold values from 0 to 31, as said below
- block_valid_rows: int32 [64], replicated, may hold values from 16 to 128, as said below
- tenant_output_row: int32 [32], replicated, may hold values from 0 to 31, as said below
Outputs:
- attention_gradient: bfloat16 [8192, 8192], P('grp', 'seq')
- grad_down: float32 [32, 64, 8192], P('grp', None, 'seq')
- grad_up: float32 [32, 64, 8192], P('grp', None, 'seq')
Inputs may be any that keep to these rules, and one draw needn't show every extreme that they name: `block_tenant_index`: the 4 blocks of one group belong to different tenants whose groups tenant_output_row[t] // 2 differ; in every draw one group keeps a tenant of one block of every group. `block_valid_rows`: in every group one block has all 128 rows valid. `tenant_output_row`: A permutation of the tenants.
All inputs are finite; a program needn't handle non-finite values.
Results may differ from a plain program's by a relative error of at most 0.0031.
Values may be sent and summed in bfloat16 or wider, within the bound.
A program may use at most 64 MiB of HBM per device.

v0:
```python
import jax
import jax.numpy as jnp
from jax import lax
from jax.sharding import PartitionSpec as P

BLOCK = 128
adapter_scale = 2.0


def shards(
    attention_output,
    output_gradient,
    output_projection_weight,
    tenant_down_factors,
    tenant_up_factors,
    block_tenant_index,
    block_valid_rows,
    tenant_output_row,
):
    group_index = lax.axis_index("grp")
    rows_group, head_cols = attention_output.shape
    col_width = output_gradient.shape[1]
    blocks = rows_group // BLOCK
    tenants = tenant_output_row.shape[0]
    place_all = jnp.sum(
        jnp.where(
            block_tenant_index[:, None] == jnp.arange(tenants, dtype=jnp.int32)[None, :],
            tenant_output_row[None, :],
            0,
        ),
        axis=1,
    )
    local_tenants = lax.dynamic_slice_in_dim(block_tenant_index, group_index * blocks, blocks)
    my_counts = lax.dynamic_slice_in_dim(block_valid_rows, group_index * blocks, blocks)
    my_places = lax.dynamic_slice_in_dim(place_all, group_index * blocks, blocks)
    positions = jnp.arange(rows_group, dtype=jnp.int32)
    block_of = positions // BLOCK
    limits = jnp.sum(
        jnp.where(
            jnp.arange(blocks, dtype=jnp.int32)[None, :] == block_of[:, None], my_counts[None, :], 0
        ),
        axis=1,
    )
    masked = jnp.where(
        (positions % BLOCK < limits)[:, None], output_gradient, jnp.zeros((), jnp.bfloat16)
    )
    contract_rows = (((1,), (1,)), ((), ()))
    weight_rows = lax.all_gather(output_projection_weight, "grp", axis=1, tiled=True)
    frozen_input_gradient = lax.dot_general(
        lax.all_gather(masked, "seq", axis=1, tiled=True),
        weight_rows,
        contract_rows,
        preferred_element_type=jnp.float32,
    )
    adapter_down_factor = tenant_down_factors[local_tenants]
    adapter_up_factor = tenant_up_factors[local_tenants]
    hidden_row_blocks = attention_output.reshape(blocks, BLOCK, head_cols)
    gradient_row_blocks = masked.reshape(blocks, BLOCK, col_width)
    down_part = jnp.einsum(
        "bkh,brh->bkr", hidden_row_blocks, adapter_down_factor, preferred_element_type=jnp.float32
    )
    grad_part = jnp.einsum(
        "ejz,elz->ejl", gradient_row_blocks, adapter_up_factor, preferred_element_type=jnp.float32
    )
    down_sum, grad_sum = lax.psum((down_part, grad_part), "seq")
    down_rank_product = down_sum.astype(jnp.bfloat16)
    rank_gradient = grad_sum.astype(jnp.bfloat16)
    adapter_branch_term = jnp.einsum(
        "wtf,wfl->wtl", rank_gradient, adapter_down_factor, preferred_element_type=jnp.float32
    ).reshape(rows_group, head_cols)
    attention_gradient = (frozen_input_gradient + adapter_scale * adapter_branch_term).astype(
        jnp.bfloat16
    )
    down_gradient_panel = adapter_scale * jnp.einsum(
        "eit,eiz->etz", rank_gradient, hidden_row_blocks, preferred_element_type=jnp.float32
    )
    up_gradient_panel = adapter_scale * jnp.einsum(
        "jlx,jln->jxn", down_rank_product, gradient_row_blocks, preferred_element_type=jnp.float32
    )
    panels = jnp.concatenate([down_gradient_panel, up_gradient_panel], axis=2)
    select = (jnp.arange(tenants, dtype=jnp.int32)[:, None] == my_places[None, :]).astype(
        jnp.float32
    )
    spread = jnp.einsum(
        "pb,brx->prx",
        select,
        panels,
        precision=lax.Precision.HIGHEST,
        preferred_element_type=jnp.float32,
    )
    summed = lax.psum_scatter(spread, "grp", scatter_dimension=0, tiled=True)
    grad_down = summed[:, :, :head_cols]
    grad_up = summed[:, :, head_cols:]
    return (attention_gradient, grad_down, grad_up)


def solution(mesh):
    placed = (
        P("grp", "seq"),
        P("grp", "seq"),
        P("seq", "grp"),
        P(None, None, "seq"),
        P(None, None, "seq"),
        P(),
        P(),
        P(),
    )
    return jax.shard_map(
        shards,
        mesh=mesh,
        in_specs=placed,
        out_specs=(P("grp", "seq"), P("grp", None, "seq"), P("grp", None, "seq")),
        check_vma=False,
    )
```

profile of v0, /device:TPU:8, one launch (start us, length us, event | category | flops | bytes accessed | tf_op | source)
XLA Modules:
  0.0 403.3 jit_solution(14572246744692483261)
XLA Ops:
  7.2 0.0 copy-start
  7.2 0.0 reduce-scatter.2.cloned.1.call-start
  7.2 0.8 dynamic_slice.9
  8.1 0.1 select_reduce_fusion.1
  8.1 0.7 compare_select_fusion
  8.9 1.1 broadcast_select_fusion
  10.0 0.0 copy-start.1
  10.0 0.0 copy-done
  10.0 0.6 gather_fusion
  10.6 0.2 fusion.16
  10.8 1.8 gather_fusion.1
  12.6 1.1 convolution_bitcast_fusion
  13.7 150.4 %all-reduce.2 = (bf16[4,128,64]{1,2,0:T(8,128)(2,1)S(1)}, bf16[4,128,64]{1,2,0:T(8,128)(2,1)S(1)}) all-reduce(f32[4,128,64]{1,2,0:T(8,128)S(1)} %fusion.16, f32[4,128,64]{1,2,0:T(8,128)S(1)} %convolution_bitcast_fusion), channel_id=1, replica_groups=mesh['grp'=16,'seq'=32] {'seq'}, use_global_device_ids=true, to_apply=%region_1.2 | all-reduce | flops 65536 | bytes 393216 | tf_op jit(solution)/shard_map/psum | solution.py:65
  164.1 0.2 convolution_multiply_fusion.1
  164.3 1.1 convolution_multiply_fusion.2
  165.4 0.8 select_reduce_fusion
  166.2 0.1 dynamic_slice.11
  166.2 0.1 pad_maximum_fusion
  166.3 2.0 fusion.1
  168.3 0.0 copy-done.1
  168.3 4.4 %copy.15 = f32[32,64,512]{2,1,0:T(8,128)} copy(f32[32,64,512]{2,0,1:T(8,128)S(1)} %fusion.1) | data formatting | bytes 8388608 | tf_op jit(solution)/shard_map/pb,brx->prx/dot_general | solution.py:84
  172.7 0.0 reduce-scatter.2.cloned.1.call-update
  172.7 0.0 all-gather.5.cloned.1.call-start
  172.8 0.7 all-gather.5.cloned.1.call-update
  173.5 0.0 all-gather.3.cloned.1.call-start
  173.5 0.7 all-gather.3.cloned.1.call-update
  174.2 0.3 convolution_multiply_fusion
  174.5 55.3 %reduce-scatter.2.cloned.1.call-done = f32[2,64,512]{2,1,0:T(8,128)} async-done(((f32[32,64,512]{2,1,0:T(8,128)}), f32[2,64,512]{2,1,0:T(8,128)}) %reduce-scatter.2.cloned.1.call-update) | async-done | bytes 262160 | tf_op jit(solution)/shard_map/reduce_scatter | solution.py:91
  229.8 1.7 fusion.15
  231.5 47.0 %all-gather.5.cloned.1.call-done = bf16[256,8192]{1,0:T(8,128)(2,1)} async-done(((bf16[256,512]{1,0:T(8,128)(2,1)}), bf16[256,8192]{1,0:T(8,128)(2,1)}) %all-gather.5.cloned.1.call-update) | async-done | bytes 4194320 | tf_op jit(solution)/shard_map/all_gather | solution.py:48
  278.4 110.7 %all-gather.3.cloned.1.call-done = bf16[512,8192]{1,0:T(8,128)(2,1)} async-done(((bf16[512,256]{1,0:T(8,128)(2,1)}), bf16[512,8192]{1,0:T(8,128)(2,1)}) %all-gather.3.cloned.1.call-update) | async-done | bytes 8388624 | tf_op jit(solution)/shard_map/all_gather | solution.py:50
  389.2 7.6 %fusion = bf16[512,256]{1,0:T(8,128)(2,1)} fusion(f32[512,256]{1,0:T(8,128)S(1)} %bitcast.24, bf16[512,8192]{1,0:T(8,128)(2,1)} %all-gather.3.cloned.1.call-done, bf16[256,8192]{1,0:T(8,128)(2,1)} %all-gather.5.cloned.1.call-done), kind=kOutput, calls=%fused_computation.4 | convolution fusion | flops 2147745792 | bytes 13369344 | tf_op jit(solution)/shard_map/dot_general | solution.py:49
  (3 shorter events, 0.0 us)
Async XLA Ops:
  7.2 2.8 copy-start
  7.2 222.6 %reduce-scatter.2.cloned.1.call-start = ((), (), s32[]{:S(2)}) async-start(), calls=%async_computation.3 | async-start | bytes 4456448 | tf_op jit(solution)/shard_map/reduce_scatter | solution.py:91
  10.0 158.3 %copy-start.1 = (bf16[512,256]{1,0:T(8,128)(2,1)}, bf16[512,256]{1,0:T(8,128)(2,1)S(1)}, u32[]{:S(2)}) copy-start(bf16[512,256]{1,0:T(8,128)(2,1)S(1)} %broadcast_select_fusion) | copy-start | bytes 786436
  172.7 105.7 %all-gather.5.cloned.1.call-start = ((), (), s32[]{:S(2)}) async-start(), calls=%async_computation.2 | async-start | bytes 4456448 | tf_op jit(solution)/shard_map/all_gather | solution.py:48
  173.5 215.7 %all-gather.3.cloned.1.call-start = ((), (), s32[]{:S(2)}) async-start(), calls=%async_computation.1 | async-start | bytes 8650752 | tf_op jit(solution)/shard_map/all_gather | solution.py:50
Sparse Core Ops, SparseCore 0:
  172.8 56.8 reduce-scatter.1
  231.9 46.4 all-gather.4
  282.0 107.0 all-gather.2
where the time goes:
time: 404 us; the launch traced here: 403 us
  waiting for transfers between devices  214 us (53%)
  blocking collectives  150 us (37%)
  between operations  13.9 us (3%)
  matrix products  12.5 us (3%)
  local copies, waits for them, and re-layouts  9.3 us (2%)
    psum x1, blocking collectives, shards(): down_sum, grad_sum = lax.psum((down_part, grad_part), 'seq')  150 us
    all_gather x1, waiting for transfers between devices, shards(): lax.all_gather(masked, 'seq', axis=1, tiled=True)  111 us
    reduce_scatter x1, waiting for transfers between devices, shards(): summed = lax.psum_scatter(spread, 'grp', scatter_dimension=0, tiled=True)  55.3 us
    all_gather x1, waiting for transfers between devices, shards(): lax.all_gather(output_projection_weight, 'grp', axis=1, tiled=True)  47 us
  transfers between devices with their start and end apart: 3, of which 3 were waited for; matrix products, arithmetic and copies ran while one was open for 0% of the time, Pallas kernels for 0%

commit v1 on v0

--- a/solution.py
+++ b/solution.py
@@ -1,3 +1,4 @@
+import functools
 import jax
 import jax.numpy as jnp
 from jax import lax
@@ -5,6 +6,21 @@
 
 BLOCK = 128
 adapter_scale = 2.0
+
+
+def _start_terms(local, peer_axis):
+    return jnp.concatenate(
+        lax.all_to_all(
+            jnp.stack([local for _ in range(lax.axis_size(peer_axis))], axis=0),
+            peer_axis,
+            split_axis=0,
+            concat_axis=0,
+        ),
+        1,
+    )
+
+
+test_numbers = functools.partial(_start_terms, peer_axis="grp")
 
 
 def shards(
@@ -45,7 +61,7 @@
         (positions % BLOCK < limits)[:, None], output_gradient, jnp.zeros((), jnp.bfloat16)
     )
     contract_rows = (((1,), (1,)), ((), ()))
-    weight_rows = lax.all_gather(output_projection_weight, "grp", axis=1, tiled=True)
+    weight_rows = test_numbers(output_projection_weight)
     frozen_input_gradient = lax.dot_general(
         lax.all_gather(masked, "seq", axis=1, tiled=True),
         weight_rows,

time: 404 us -> 325 us (0.80)
  the two profiles are of different devices: /device:TPU:8 before, /device:TPU:29 now
where the time goes in v1:
time: 325 us
  waiting for transfers between devices  128 us (39%)
  blocking collectives  118 us (36%)
  starting transfers between devices  35.8 us (11%)
  between operations  15.6 us (5%)
  matrix products  12.5 us (4%)
  local copies, waits for them, and re-layouts  12.1 us (4%)
    reduce_scatter x1, waiting for transfers between devices, shards(): summed = lax.psum_scatter(spread, 'grp', scatter_dimension=0, tiled=True)  127 us
    psum x1, blocking collectives, shards(): down_sum, grad_sum = lax.psum((down_part, grad_part), 'seq')  118 us
    all_to_all x1, starting transfers between devices, _start_terms(): lax.all_to_all(jnp.stack([local for _ in range(lax.axis_size(peer_axis))]...  35.7 us
    dot_general x1, matrix products, shards(): lax.dot_general(lax.all_gather(masked, 'seq', axis=1, tiled=True), weight...  7.61 us
  transfers between devices with their start and end apart: 3, of which 1 were waited for; matrix products, arithmetic and copies ran while one was open for 1% of the time, Pallas kernels for 0%

profile of v1, /device:TPU:29, one launch (start us, length us, event | category | flops | bytes accessed | tf_op | source)
XLA Modules:
  0.0 324.8 jit_solution(16980761010399063740)
XLA Ops:
  8.0 0.0 copy-start
  8.0 0.0 reduce-scatter.2.cloned.1.call-start
  8.1 0.8 dynamic_slice.9
  8.9 0.7 compare_select_fusion
  9.6 0.8 select_reduce_fusion
  10.4 0.1 dynamic_slice.11
  10.5 0.1 select_reduce_fusion.1
  10.6 0.0 copy-done
  10.6 0.6 gather_fusion.1
  11.1 1.8 gather_fusion
  12.9 1.1 convolution_bitcast_fusion
  14.1 1.1 broadcast_select_fusion
  15.2 0.0 copy-start.1
  15.2 0.2 fusion.16
  15.4 118.0 %all-reduce.2 = (bf16[4,128,64]{1,2,0:T(8,128)(2,1)S(1)}, bf16[4,128,64]{1,2,0:T(8,128)(2,1)S(1)}) all-reduce(f32[4,128,64]{1,2,0:T(8,128)S(1)} %fusion.16, f32[4,128,64]{1,2,0:T(8,128)S(1)} %convolution_bitcast_fusion), channel_id=1, replica_groups=mesh['grp'=16,'seq'=32] {'seq'}, use_global_device_ids=true, to_apply=%region_1.2 | all-reduce | flops 65536 | bytes 393216 | tf_op jit(solution)/shard_map/psum | solution.py:81
  133.4 0.2 convolution_multiply_fusion.1
  133.6 1.1 convolution_multiply_fusion.2
  134.7 0.1 pad_maximum_fusion
  134.8 2.0 fusion.1
  136.8 4.4 %copy.21 = f32[32,64,512]{2,1,0:T(8,128)} copy(f32[32,64,512]{2,0,1:T(8,128)S(1)} %fusion.1) | data formatting | bytes 8388608 | tf_op jit(solution)/shard_map/pb,brx->prx/dot_general | solution.py:100
  141.1 0.0 copy-done.1
  141.1 0.0 copy-start.2
  141.1 0.0 reduce-scatter.2.cloned.1.call-update
  141.2 0.0 all-gather.2.cloned.1.call-start
  141.2 0.5 all-gather.2.cloned.1.call-update
  141.7 0.3 copy-done.2
  142.1 0.1 copy.19
  142.2 2.3 stack.2
  144.6 35.7 %all-to-all-start = ((bf16[16,256,512]{1,2,0:T(8,128)(2,1)}), bf16[16,256,512]{1,2,0:T(8,128)(2,1)}, u32[]{:S(2)}, u32[]{:S(2)}) async-start(bf16[16,256,512]{1,2,0:T(8,128)(2,1)} %stack.2), calls=%async_computation | async-start | bytes 8388608 | tf_op jit(solution)/shard_map/all_to_all | solution.py:13
  180.3 0.3 convolution_multiply_fusion
  180.6 127.4 %reduce-scatter.2.cloned.1.call-done = f32[2,64,512]{2,1,0:T(8,128)} async-done(((f32[32,64,512]{2,1,0:T(8,128)}), f32[2,64,512]{2,1,0:T(8,128)}) %reduce-scatter.2.cloned.1.call-update) | async-done | bytes 262160 | tf_op jit(solution)/shard_map/reduce_scatter | solution.py:107
  308.0 1.7 fusion.15
  309.7 0.0 all-to-all-done
  309.7 0.0 all-gather.2.cloned.1.call-done
  309.7 7.6 %fusion = bf16[512,256]{1,0:T(8,128)(2,1)} fusion(f32[512,256]{1,0:T(8,128)S(1)} %bitcast.27, bf16[512,8192]{1,0:T(8,128)(2,1)} %all-gather.2.cloned.1.call-done, bf16[256,8192]{0,1:T(8,128)(2,1)} %bitcast.1), kind=kOutput, calls=%fused_computation.4 | convolution fusion | flops 2147745792 | bytes 13369344 | tf_op jit(solution)/shard_map/dot_general | solution.py:65
  (3 shorter events, 0.0 us)
Async XLA Ops:
  8.0 2.6 copy-start
  8.0 300.0 %reduce-scatter.2.cloned.1.call-start = ((), (), s32[]{:S(2)}) async-start(), calls=%async_computation.3 | async-start | bytes 4456448 | tf_op jit(solution)/shard_map/reduce_scatter | solution.py:107
  15.2 126.0 %copy-start.1 = (bf16[512,256]{1,0:T(8,128)(2,1)}, bf16[512,256]{1,0:T(8,128)(2,1)S(1)}, u32[]{:S(2)}) copy-start(bf16[512,256]{1,0:T(8,128)(2,1)S(1)} %broadcast_select_fusion) | copy-start | bytes 786436
  141.1 1.0 copy-start.2
  141.2 168.5 %all-gather.2.cloned.1.call-start = ((), (), s32[]{:S(2)}) async-start(), calls=%async_computation.2 | async-start | bytes 8650752 | tf_op jit(solution)/shard_map/all_gather | solution.py:66
  144.6 165.1 %all-to-all-start = ((bf16[16,256,512]{1,2,0:T(8,128)(2,1)}), bf16[16,256,512]{1,2,0:T(8,128)(2,1)}, u32[]{:S(2)}, u32[]{:S(2)}) async-start(bf16[16,256,512]{1,2,0:T(8,128)(2,1)} %stack.2), calls=%async_computation | async-start | bytes 8388608 | tf_op jit(solution)/shard_map/all_to_all | solution.py:13
Sparse Core Ops, SparseCore 0:
  141.3 166.6 reduce-scatter.1
Sparse Core Ops, SparseCore 1:
  145.3 130.7 all-gather.1
